TPU v7x, 256 devices: a whole 4x4x8 slice. The times are simulated.
256 devices in a mesh: group: 8 (over z_hi, core), tensor: 8 (over y, z_lo), seq: 4 (over x).
Axes of the slice: x: 4, y: 4, z: 8 (z_hi: 4, z_lo: 2; z = z_hi * 2 + z_lo), core: 2. Of those that a mesh axis runs over, the one named last changes fastest.
Arguments:
- patches: bfloat16 [8192, 1280], P(('group', 'tensor', 'seq')), may hold values from -6 to 6
- enc_gain: float32 [1280], replicated, may hold values from 0.1 to 1.9
- enc_qkv: bfloat16 [3, 1280, 1280], P(None, None, 'tensor')
- enc_out: bfloat16 [1280, 1280], P('tensor'), may hold values from -0.15625 to 0.15625
- cross_kv: bfloat16 [1280, 2048], P(None, 'tensor'), may hold values from -0.15625 to 0.15625
- key_gain: float32 [128], replicated, may hold values from 0.1 to 1.9
- dec_hidden: bfloat16 [4096, 8192], P(('group', 'seq')), may hold values from -6 to 6
- dec_gain: float32 [8192], replicated, may hold values from 0.1 to 1.9
- query_weight: bfloat16 [8192, 4096], P(None, 'tensor'), may hold values from -0.0625 to 0.0625
- query_gain: float32 [128], replicated, may hold values from 1.5 to 3
- image_of_row: int32 [4096], P(('group', 'seq')), may hold values from 0 to 3
- valid_count: int32 [4096], P(('group', 'seq')), may hold values from 1 to 2048, as said below
Outputs:
- decoded: bfloat16 [4096, 4096], P(('group', 'seq'), 'tensor')
Inputs may be any that keep to these rules, and one draw needn't show every extreme that they name: `valid_count`: every draw has a row reading a whole image and a row reading one patch.
All inputs are finite; a program needn't handle non-finite values.
Results may differ from a plain program's by a relative error of at most 0.028.
The roundings to bfloat16 on the way count: a program that leaves them out, or rounds other values in their place, can miss the bound.
Values may be sent and summed in bfloat16 or wider, within the bound.
No kernel may reach another device: no remote copies, remote signals or barrier semaphores. Data moves between devices by JAX's collectives and lax.ppermute only.
A program may use at most 128 MiB of HBM per device.

v0:
```python
import math
import jax
import jax.numpy as jnp
from jax import lax
from jax.sharding import PartitionSpec as P

EHD = 80
HD = 128
IMAGES = 4
EPSILON = 1e-05


def layer_norm(values, gain_vector):
    mean_value = jnp.mean(values, axis=-1, keepdims=True)
    centered = values - mean_value
    variance = jnp.mean(centered * centered, axis=-1, keepdims=True)
    return centered * lax.rsqrt(variance + EPSILON) * gain_vector


def rms_norm(values, gain_vector):
    square_mean = jnp.mean(values * values, axis=-1, keepdims=True)
    return values * lax.rsqrt(square_mean + EPSILON) * gain_vector


def on_device(
    patches,
    enc_gain,
    enc_qkv,
    enc_out,
    cross_kv,
    key_gain,
    dec_hidden,
    dec_gain,
    query_weight,
    query_gain,
    image_of_row,
    valid_count,
):
    tensor_count = lax.axis_size("tensor")
    seq_count = lax.axis_size("seq")
    patch_rows = patches.shape[0]
    deal_block = patch_rows * seq_count
    gathered = lax.all_gather(patches, "tensor", axis=0, tiled=True)
    row_count = gathered.shape[0]
    normed = layer_norm(gathered.astype(jnp.float32), enc_gain).astype(jnp.bfloat16)
    local_width = enc_qkv.shape[2]
    local_heads = local_width // EHD
    query_part = (
        jnp.dot(normed, enc_qkv[0], preferred_element_type=jnp.float32)
        .astype(jnp.bfloat16)
        .reshape(row_count, local_heads, EHD)
    )
    key_part = jnp.dot(normed, enc_qkv[1], preferred_element_type=jnp.float32).astype(jnp.bfloat16)
    value_part = jnp.dot(normed, enc_qkv[2], preferred_element_type=jnp.float32).astype(
        jnp.bfloat16
    )

    def patch_number(gathered_index):
        shard_number = gathered_index // row_count
        within = gathered_index % row_count
        source_tensor = within // patch_rows
        source_row = within % patch_rows
        source_group = shard_number // seq_count
        source_seq = shard_number % seq_count
        return (
            (source_group * tensor_count + source_tensor) * seq_count + source_seq
        ) * patch_rows + source_row

    def image_number(patch_index):
        return patch_index // deal_block % IMAGES

    own_index = jnp.arange(row_count, dtype=jnp.int32)
    own_shard = lax.axis_index("group") * seq_count + lax.axis_index("seq")
    query_image = image_number(patch_number(own_shard * row_count + own_index))
    running_max = jnp.full((local_heads, row_count), -1e30, jnp.float32)
    key_shard = lax.all_gather(key_part, ("group", "seq"), axis=0, tiled=True)
    value_shard = lax.all_gather(value_part, ("group", "seq"), axis=0, tiled=True)
    piece_rows = key_shard.shape[0]
    key_index = jnp.arange(piece_rows, dtype=jnp.int32)
    key_image = image_number(patch_number(key_index))
    same_image = (query_image[:, None] == key_image[None, :])[None]
    key_heads = key_shard.reshape(piece_rows, local_heads, EHD)
    value_heads = value_shard.reshape(piece_rows, local_heads, EHD)
    scores = jnp.einsum(
        "rhd,khd->hrk", query_part, key_heads, preferred_element_type=jnp.float32
    ) / math.sqrt(EHD)
    masked = jnp.where(same_image, scores, jnp.full_like(scores, -1e30))
    new_max = jnp.maximum(running_max, jnp.max(masked, axis=-1))
    weights = jnp.where(same_image, jnp.exp(scores - new_max[..., None]), jnp.zeros_like(scores))
    new_sum = jnp.sum(weights, axis=-1)
    new_mix = jnp.einsum(
        "hrk,khd->hrd",
        weights.astype(jnp.bfloat16),
        value_heads,
        preferred_element_type=jnp.float32,
    )
    folded = (new_max, new_sum, new_mix)
    final_max, final_sum, final_mix = folded
    attended = (final_mix / final_sum[..., None]).astype(jnp.bfloat16)
    attended = attended.transpose(1, 0, 2).reshape(row_count, local_width)
    total_out = lax.psum(
        jnp.dot(attended, enc_out, preferred_element_type=jnp.float32).astype(jnp.bfloat16),
        "tensor",
    ).astype(jnp.float32)
    encoded = (gathered.astype(jnp.float32) + total_out).astype(jnp.bfloat16)
    kv_local = cross_kv.shape[1] // (2 * HD)
    cross_proj = jnp.dot(encoded, cross_kv, preferred_element_type=jnp.float32).reshape(
        row_count, kv_local, 2, HD
    )
    cross_keys = rms_norm(cross_proj[:, :, 0], key_gain)
    kv_slab = (
        jnp.stack([cross_keys, cross_proj[:, :, 1]], axis=2)
        .astype(jnp.bfloat16)
        .reshape(row_count, kv_local * 2 * HD)
    )
    every_slab = lax.all_gather(kv_slab, ("group", "seq"), axis=0, tiled=True)
    dec_rows = dec_hidden.shape[0]
    dec_normed = rms_norm(dec_hidden.astype(jnp.float32), dec_gain).astype(jnp.bfloat16)
    query_local = query_weight.shape[1] // HD
    group_size = query_local // kv_local
    queries = jnp.dot(dec_normed, query_weight, preferred_element_type=jnp.float32).reshape(
        dec_rows, query_local, HD
    )
    queries = (rms_norm(queries, query_gain) / math.sqrt(HD)).astype(jnp.bfloat16)
    queries = queries.reshape(dec_rows, kv_local, group_size, HD)
    slab_rows = every_slab.shape[0]
    slab_view = every_slab.reshape(slab_rows, kv_local, 2, HD)
    patch_index = patch_number(jnp.arange(slab_rows, dtype=jnp.int32))
    slab_image = image_number(patch_index)
    slab_position = patch_index // (deal_block * IMAGES) * deal_block + patch_index % deal_block
    allowed = (slab_image[None, :] == image_of_row[:, None]) & (
        slab_position[None, :] < valid_count[:, None]
    )
    scores = jnp.einsum(
        "rgqd,kgd->gqrk", queries, slab_view[:, :, 0], preferred_element_type=jnp.float32
    )
    weights = jnp.where(allowed[None, None], jnp.exp(scores), jnp.zeros_like(scores))
    weight_sum = jnp.sum(weights, axis=-1)
    mixture = jnp.einsum(
        "gqrk,kgd->rgqd",
        weights.astype(jnp.bfloat16),
        slab_view[:, :, 1],
        preferred_element_type=jnp.float32,
    )
    result = mixture / weight_sum.transpose(2, 0, 1)[..., None]
    return result.astype(jnp.bfloat16).reshape(dec_rows, query_local * HD)


def solution(mesh):
    in_specs = (
        P(("group", "tensor", "seq"), None),
        P(),
        P(None, None, "tensor"),
        P("tensor", None),
        P(None, "tensor"),
        P(),
        P(("group", "seq"), None),
        P(),
        P(None, "tensor"),
        P(),
        P(("group", "seq")),
        P(("group", "seq")),
    )
    out_specs = P(("group", "seq"), "tensor")
    return jax.shard_map(
        on_device, mesh=mesh, in_specs=in_specs, out_specs=out_specs, check_vma=False
    )
```

profile of v0, /device:TPU:1, one launch (start us, length us, event | category | flops | bytes accessed | tf_op | source)
XLA Modules:
  0.0 340.4 jit_solution(16745044006763906302)
XLA Ops:
  6.5 0.0 copy-start
  6.5 0.0 copy-start.9
  6.5 0.0 all-gather.4.cloned.1.call-start
  6.5 26.6 %all_gather.12 = bf16[256,1280]{1,0:T(8,128)(2,1)S(1)} all-gather(bf16[32,1280]{1,0:T(8,128)(2,1)} %param.12), channel_id=1, replica_groups=mesh['group'=8,'tensor'=8,'seq'=4] {'tensor'}, dimensions={0}, use_global_device_ids=true | all-gather | bytes 737280 | tf_op jit(solution)/shard_map/all_gather | solution.py:43
  33.1 0.2 convert_reduce_fusion
  33.3 0.3 fusion.22
  33.6 1.0 fusion.24
  34.6 2.0 convolution_convert_fusion.2
  36.6 0.0 all-gather.4.cloned.1.call-update
  36.6 0.0 all-gather.6.cloned.1.call-start
  36.7 0.0 copy-done.9
  36.7 1.0 convolution_convert_fusion.1
  37.7 0.0 all-gather.6.cloned.1.call-update
  37.7 0.0 all-reduce.2.cloned.1.call-start
  37.8 0.1 add_select_fusion.2
  37.9 0.4 convolution_convert_fusion.3
  38.3 1.2 broadcast_compare_fusion
  39.5 62.9 %all-gather.4.cloned.1.call-done = bf16[8192,160]{0,1:T(8,128)(2,1)} async-done(((bf16[256,160]{0,1:T(8,128)(2,1)}), bf16[8192,160]{0,1:T(8,128)(2,1)}) %all-gather.4.cloned.1.call-update) | async-done | bytes 2621456 | tf_op jit(solution)/shard_map/all_gather | solution.py:76
  102.4 5.6 %select_reduce_fusion = (f32[2,256]{1,0:T(2,128)S(1)}, f32[2,256,8192]{2,1,0:T(8,128)S(1)}) fusion(pred[256,8192]{1,0:T(8,128)(4,1)S(1)} %broadcast_compare_fusion, bf16[256,2,80]{0,2,1:T(8,128)(2,1)S(1)} %bitcast.128, bf16[8192,2,80]{0,2,1:T(8,128)(2,1)} %bitcast.126), kind=kOutput, calls=%fused_computation.2 | convolution fusion | flops 683671040 | bytes 21579776 | tf_op jit(solution)/shard_map/rhd,khd->hrk/dot_general | solution.py:84
  108.0 0.0 copy-start.1
  108.0 5.7 %copy-done.1 = f32[2,256,8192]{2,1,0:T(8,128)} copy-done((f32[2,256,8192]{2,1,0:T(8,128)}, f32[2,256,8192]{2,1,0:T(8,128)S(1)}, u32[]{:S(2)}) %copy-start.1) | copy-done | bytes 16777240
  113.7 4.8 %fusion.2 = f32[2,256]{1,0:T(2,128)S(1)} fusion(f32[2,256,8192]{2,1,0:T(8,128)S(1)} %get-tuple-element.6, f32[2,256]{1,0:T(2,128)S(1)} %broadcast_maximum_fusion, pred[256,8192]{1,0:T(8,128)(4,1)S(1)} %broadcast_compare_fusion), kind=kLoop, calls=%fused_computation.5 | loop fusion | flops 16776704 | bytes 18878464 | tf_op jit(solution)/shard_map/reduce_sum | solution.py:90
  118.5 41.9 %all-gather.6.cloned.1.call-done = bf16[8192,160]{0,1:T(8,128)(2,1)} async-done(((bf16[256,160]{0,1:T(8,128)(2,1)}), bf16[8192,160]{0,1:T(8,128)(2,1)}) %all-gather.6.cloned.1.call-update) | async-done | bytes 2621456 | tf_op jit(solution)/shard_map/all_gather | solution.py:77
  160.4 0.0 copy-start.3
  160.4 8.5 %fusion.35 = bf16[256,2,80]{0,2,1:T(8,128)(2,1)S(1)} fusion(bf16[8192,2,80]{0,2,1:T(8,128)(2,1)} %bitcast.127, f32[2,256,8192]{2,1,0:T(8,128)} %copy-done.1, f32[2,256]{1,0:T(2,128)S(1)} %broadcast_maximum_fusion, pred[256,8192]{1,0:T(8,128)(4,1)S(1)} %broadcast_compare_fusion, f32[256,2]{0,1:T(2,128)S(1)} %bitcast.123), kind=kOutput, calls=%fused_computation.42 | convolution fusion | flops 687947776 | bytes 21581824 | tf_op jit(solution)/shard_map/hrk,khd->hrd/dot_general | solution.py:91
  168.9 0.0 copy-start.6
  168.9 0.0 copy-start.2
  168.9 0.0 copy-start.10
  169.0 0.0 copy-done.3
  169.0 1.2 convolution_convert_fusion
  170.2 0.0 all-reduce.2.cloned.1.call-update
  170.2 0.2 all-gather.8.cloned.1.call-start
  170.4 74.0 %all-reduce.2.cloned.1.call-done = bf16[256,1280]{1,0:T(8,128)(2,1)} async-done(((bf16[256,1280]{1,0:T(8,128)(2,1)}), bf16[256,1280]{1,0:T(8,128)(2,1)}) %all-reduce.2.cloned.1.call-update) | async-done | bytes 655376 | tf_op jit(solution)/shard_map/psum | solution.py:101
  244.4 0.0 copy-done
  244.4 1.5 fusion.44
  246.0 0.0 copy-done.6
  246.0 0.1 multiply_convert_fusion
  246.1 0.7 pad_maximum_fusion
  246.8 0.0 all-gather.8.cloned.1.call-update
  246.8 0.0 copy-done.2
  246.8 0.5 fusion.12
  247.3 0.0 copy-done.10
  247.3 0.0 copy-start.7
  247.3 0.0 copy-start.4
  247.4 0.0 copy-start.5
  247.4 5.4 %fusion.100 = (f32[128,512]{1,0:T(8,128)S(1)}, f32[128,512]{1,0:T(8,128)}) fusion(bf16[8192,512]{1,0:T(8,128)(2,1)} %param.20, bf16[128,8192]{1,0:T(8,128)(2,1)S(1)} %copy-done.2, f32[8192]{0:T(1024)S(1)} %copy-done.10, f32[128]{0:T(128)S(1)} %add_rsqrt_fusion.3), kind=kOutput, calls=%fused_computation.160 | convolution fusion | flops 1078001664 | bytes 11043328 | tf_op jit(solution)/shard_map/dot_general | solution.py:121
  252.8 0.1 mul.214
  252.9 0.2 reduce_sum.70
  253.1 0.1 fusion.73
  253.1 0.0 copy-done.7
  253.2 0.0 copy-done.4
  253.2 0.0 copy-done.5
  253.2 2.8 compare_and_fusion
  256.0 58.9 %all-gather.8.cloned.1.call-done = bf16[8192,256]{0,1:T(8,128)(2,1)} async-done(((bf16[256,256]{0,1:T(8,128)(2,1)}), bf16[8192,256]{0,1:T(8,128)(2,1)}) %all-gather.8.cloned.1.call-update) | async-done | bytes 4194320 | tf_op jit(solution)/shard_map/all_gather | solution.py:116
  314.9 0.2 mul.215
  315.1 0.0 copy-start.8
  315.1 10.6 %fusion = (f32[4,128]{1,0:T(4,128)S(1)}, f32[8192,128,4]{1,0,2:T(8,128)}) fusion(pred[128,8192]{0,1:T(8,128)(4,1)S(1)} %compare_and_fusion, bf16[8192,1,2,128]{0,3,2,1:T(8,128)(2,1)} %bitcast.124, f32[128,512]{1,0:T(8,128)} %get-tuple-element.8, f32[16,8,4,128]{3,2,1,0:T(4,128)S(1)} %bitcast.120, f32[512]{0:T(512)S(1)} %broadcast_bitcast_fusion), kind=kOutput, calls=%fused_computation.3 | convolution fusion | flops 1082392064 | bytes 20451328 | tf_op jit(solution)/shard_map/rgqd,kgd->gqrk/dot_general | solution.py:134
  325.7 0.0 copy-done.8
  325.7 7.4 %fusion.41 = bf16[128,1,4,128]{0,3,2,1:T(8,128)(2,1)S(1)} fusion(f32[8192,128,4]{1,0,2:T(8,128)} %get-tuple-element.10, pred[128,8192]{0,1:T(8,128)(4,1)S(1)} %compare_and_fusion, bf16[8192,1,2,128]{0,3,2,1:T(8,128)(2,1)S(1)} %bitcast.125, f32[128,4]{0,1:T(4,128)S(1)} %bitcast.129), kind=kOutput, calls=%fused_computation.44 | convolution fusion | flops 1082261504 | bytes 20056064 | tf_op jit(solution)/shard_map/gqrk,kgd->rgqd/dot_general | solution.py:139
  333.1 0.8 copy.31
  (10 shorter events, 0.1 us)
Async XLA Ops:
  6.5 237.9 %copy-start = (bf16[1280,256]{1,0:T(8,128)(2,1)S(1)}, bf16[1280,256]{1,0:T(8,128)(2,1)}, u32[]{:S(2)}) copy-start(bf16[1280,256]{1,0:T(8,128)(2,1)} %param.16) | copy-start | bytes 1966084
  6.5 30.2 %copy-start.9 = (bf16[3,1280,160]{1,2,0:T(8,128)(2,1)S(1)}, bf16[3,1280,160]{1,2,0:T(8,128)(2,1)}, u32[]{:S(2)}) copy-start(bf16[3,1280,160]{1,2,0:T(8,128)(2,1)} %param.14) | copy-start | bytes 3686404
  6.5 95.9 %all-gather.4.cloned.1.call-start = ((), (), s32[]{:S(2)}) async-start(), calls=%async_computation | async-start | bytes 2703360 | tf_op jit(solution)/shard_map/all_gather | solution.py:76
  36.6 123.8 %all-gather.6.cloned.1.call-start = ((), (), s32[]{:S(2)}) async-start(), calls=%async_computation.1 | async-start | bytes 2703360 | tf_op jit(solution)/shard_map/all_gather | solution.py:77
  37.7 206.7 %all-reduce.2.cloned.1.call-start = ((), (), s32[]{:S(2)}) async-start(), calls=%async_computation.2 | async-start | bytes 1310720 | tf_op jit(solution)/shard_map/psum | solution.py:101
  108.0 5.7 %copy-start.1 = (f32[2,256,8192]{2,1,0:T(8,128)}, f32[2,256,8192]{2,1,0:T(8,128)S(1)}, u32[]{:S(2)}) copy-start(f32[2,256,8192]{2,1,0:T(8,128)S(1)} %get-tuple-element.6) | copy-start | bytes 50331652
  160.4 8.6 %copy-start.3 = (bf16[160,1280]{1,0:T(8,128)(2,1)S(1)}, bf16[160,1280]{1,0:T(8,128)(2,1)}, u32[]{:S(2)}) copy-start(bf16[160,1280]{1,0:T(8,128)(2,1)} %param.15) | copy-start | bytes 1228804
  168.9 77.1 %copy-start.6 = (f32[128]{0:T(128)S(1)}, f32[128]{0:T(128)}, u32[]{:S(2)}) copy-start(f32[128]{0:T(128)} %param.17) | copy-start | bytes 1540
  168.9 77.9 %copy-start.2 = (bf16[128,8192]{1,0:T(8,128)(2,1)S(1)}, bf16[128,8192]{1,0:T(8,128)(2,1)}, u32[]{:S(2)}) copy-start(bf16[128,8192]{1,0:T(8,128)(2,1)} %param.18) | copy-start | bytes 6291460
  168.9 78.4 %copy-start.10 = (f32[8192]{0:T(1024)S(1)}, f32[8192]{0:T(1024)}, u32[]{:S(2)}) copy-start(f32[8192]{0:T(1024)} %param.19) | copy-start | bytes 98308
  170.2 144.7 %all-gather.8.cloned.1.call-start = ((), (), s32[]{:S(2)}) async-start(), calls=%async_computation.3 | async-start | bytes 4325376 | tf_op jit(solution)/shard_map/all_gather | solution.py:116
  247.3 5.8 %copy-start.7 = (f32[128]{0:T(128)S(1)}, f32[128]{0:T(128)}, u32[]{:S(2)}) copy-start(f32[128]{0:T(128)} %param.21) | copy-start | bytes 1540
  247.3 5.8 %copy-start.4 = (s32[128]{0:T(128)S(1)}, s32[128]{0:T(128)}, u32[]{:S(2)}) copy-start(s32[128]{0:T(128)} %param.23) | copy-start | bytes 1540
  247.4 5.8 %copy-start.5 = (s32[128]{0:T(128)S(1)}, s32[128]{0:T(128)}, u32[]{:S(2)}) copy-start(s32[128]{0:T(128)} %param.22) | copy-start | bytes 1540
  315.1 10.6 %copy-start.8 = (bf16[8192,256]{0,1:T(8,128)(2,1)S(1)}, bf16[8192,256]{0,1:T(8,128)(2,1)}, u32[]{:S(2)}) copy-start(bf16[8192,256]{0,1:T(8,128)(2,1)} %all-gather.8.cloned.1.call-done) | copy-start | bytes 12582916
Sparse Core Ops, SparseCore 0:
  36.8 65.6 all-gather.3
  104.9 55.4 all-gather.5
  170.3 74.0 all-reduce.1
  246.9 67.8 all-gather.7
where the time goes:
time: 341 us; the launch traced here: 340 us
  waiting for transfers between devices  238 us (70%)
  matrix products  43.6 us (13%)
  blocking collectives  26.6 us (8%)
  between operations  13.4 us (4%)
  other arithmetic  11.9 us (3%)
  local copies, waits for them, and re-layouts  6.82 us (2%)
    psum x1, waiting for transfers between devices, on_device(): lax.psum(jnp.dot(attended, enc_out, preferred_element_type=jnp.float32).a...  74 us
    all_gather x1, waiting for transfers between devices, on_device(): key_shard = lax.all_gather(key_part, ('group', 'seq'), axis=0, tiled=True)  62.9 us
    all_gather x1, waiting for transfers between devices, on_device(): every_slab = lax.all_gather(kv_slab, ('group', 'seq'), axis=0, tiled=True)  58.9 us
    all_gather x1, waiting for transfers between devices, on_device(): lax.all_gather(value_part, ('group', 'seq'), axis=0, tiled=True)  41.9 us
    all_gather x1, blocking collectives, on_device(): gathered = lax.all_gather(patches, 'tensor', axis=0, tiled=True)  26.6 us
    dot_general x1, matrix products, on_device(): jnp.einsum('rgqd,kgd->gqrk', queries, slab_view[:, :, 0], preferred_eleme...  10.6 us
    dot_general x1, matrix products, on_device(): jnp.einsum('hrk,khd->hrd', weights.astype(jnp.bfloat16), value_heads, pre...  8.5 us
    dot_general x1, matrix products, on_device(): jnp.einsum('gqrk,kgd->rgqd', weights.astype(jnp.bfloat16), slab_view[:, :...  7.39 us
  transfers between devices with their start and end apart: 4, of which 4 were waited for; matrix products, arithmetic and copies ran while one was open for 7% of the time, Pallas kernels for 0%

commit v1 on v0

--- a/solution.py
+++ b/solution.py
@@ -113,7 +113,12 @@
         .astype(jnp.bfloat16)
         .reshape(row_count, kv_local * 2 * HD)
     )
-    every_slab = lax.all_gather(kv_slab, ("group", "seq"), axis=0, tiled=True)
+    every_slab = jnp.concatenate(
+        lax.all_to_all(
+            jnp.stack([kv_slab] * lax.axis_size(("group", "seq"))), ("group", "seq"), 0, 0
+        ),
+        axis=0,
+    )
     dec_rows = dec_hidden.shape[0]
     dec_normed = rms_norm(dec_hidden.astype(jnp.float32), dec_gain).astype(jnp.bfloat16)
     query_local = query_weight.shape[1] // HD

time: 341 us -> 399 us (1.17)
  waiting for transfers between devices: 238 us -> 268 us
  local copies, waits for them, and re-layouts: 6.82 us -> 23.2 us
  starting transfers between devices: 0.31 us -> 14.5 us
    all_to_all x0 -> x1, waiting for transfers between devices: none -> 88.4 us  [on_device(): lax.all_to_all(jnp.stack([kv_slab] * lax.axis_size(('group', 'seq'))), ('...]
    all_gather x1 -> x0, waiting for transfers between devices: 58.9 us -> none  [on_device(): every_slab = lax.all_gather(kv_slab, ('group', 'seq'), axis=0, tiled=True)]
    all_to_all x0 -> x1, starting transfers between devices: none -> 14.4 us  [on_device(): lax.all_to_all(jnp.stack([kv_slab] * lax.axis_size(('group', 'seq'))), ('...]
    another operation x0 -> x2, local copies, waits for them, and re-layouts: none -> 9.86 us  [the longest x1 7.41 us: on_device(): slab_view = every_slab.reshape(slab_rows, kv_local, 2, HD)]
    all_to_all x0 -> x1, local copies, waits for them, and re-layouts: none -> 6.53 us  [on_device(): lax.all_to_all(jnp.stack([kv_slab] * lax.axis_size(('group', 'seq'))), ('...]
  transfers between devices with their start and end apart: 4 -> 4, of which waited for: 4 -> 4; matrix products, arithmetic and copies ran while one was open for 7% -> 5% of each run, Pallas kernels for 0% -> 0%
where the time goes in v1:
time: 399 us; the launch traced here: 398 us
  waiting for transfers between devices  268 us (67%)
  matrix products  42 us (11%)
  blocking collectives  26.6 us (7%)
  local copies, waits for them, and re-layouts  23.2 us (6%)
  starting transfers between devices  14.5 us (4%)
  between operations  13.4 us (3%)
  other arithmetic  11.3 us (3%)
    all_to_all x1, waiting for transfers between devices, on_device(): lax.all_to_all(jnp.stack([kv_slab] * lax.axis_size(('group', 'seq'))), ('...  88.4 us
    psum x1, waiting for transfers between devices, on_device(): lax.psum(jnp.dot(attended, enc_out, preferred_element_type=jnp.float32).a...  74.2 us
    all_gather x1, waiting for transfers between devices, on_device(): key_shard = lax.all_gather(key_part, ('group', 'seq'), axis=0, tiled=True)  62.9 us
    all_gather x1, waiting for transfers between devices, on_device(): lax.all_gather(value_part, ('group', 'seq'), axis=0, tiled=True)  41.9 us
    all_gather x1, blocking collectives, on_device(): gathered = lax.all_gather(patches, 'tensor', axis=0, tiled=True)  26.6 us
    all_to_all x1, starting transfers between devices, on_device(): lax.all_to_all(jnp.stack([kv_slab] * lax.axis_size(('group', 'seq'))), ('...  14.4 us
    dot_general x1, matrix products, on_device(): jnp.einsum('rgqd,kgd->gqrk', queries, slab_view[:, :, 0], preferred_eleme...  9.56 us
    dot_general x1, matrix products, on_device(): jnp.einsum('hrk,khd->hrd', weights.astype(jnp.bfloat16), value_heads, pre...  8.5 us
  transfers between devices with their start and end apart: 4, of which 4 were waited for; matrix products, arithmetic and copies ran while one was open for 5% of the time, Pallas kernels for 0%

profile of v1, /device:TPU:1, one launch (start us, length us, event | category | flops | bytes accessed | tf_op | source)
XLA Modules:
  0.0 398.5 jit_solution(12006192971372563257)
XLA Ops:
  6.5 0.0 copy-start
  6.5 0.0 copy-start.10
  6.5 0.0 all-gather.3.cloned.1.call-start
  6.5 26.6 %all_gather.9 = bf16[256,1280]{1,0:T(8,128)(2,1)S(1)} all-gather(bf16[32,1280]{1,0:T(8,128)(2,1)} %param.12), channel_id=1, replica_groups=mesh['group'=8,'tensor'=8,'seq'=4] {'tensor'}, dimensions={0}, use_global_device_ids=true | all-gather | bytes 737280 | tf_op jit(solution)/shard_map/all_gather | solution.py:43
  33.1 0.2 convert_reduce_fusion
  33.3 0.3 fusion.22
  33.6 1.0 fusion.24
  34.6 2.0 convolution_convert_fusion.2
  36.6 0.0 all-gather.3.cloned.1.call-update
  36.6 0.0 all-gather.5.cloned.1.call-start
  36.7 0.0 copy-done.10
  36.7 1.0 convolution_convert_fusion.1
  37.7 0.0 all-gather.5.cloned.1.call-update
  37.7 0.0 all-reduce.2.cloned.1.call-start
  37.8 0.1 add_select_fusion.2
  37.9 0.4 convolution_convert_fusion.3
  38.3 1.2 broadcast_compare_fusion
  39.5 62.9 %all-gather.3.cloned.1.call-done = bf16[8192,160]{0,1:T(8,128)(2,1)} async-done(((bf16[256,160]{0,1:T(8,128)(2,1)}), bf16[8192,160]{0,1:T(8,128)(2,1)}) %all-gather.3.cloned.1.call-update) | async-done | bytes 2621456 | tf_op jit(solution)/shard_map/all_gather | solution.py:76
  102.4 5.6 %select_reduce_fusion = (f32[2,256]{1,0:T(2,128)S(1)}, f32[2,256,8192]{2,1,0:T(8,128)S(1)}) fusion(pred[256,8192]{1,0:T(8,128)(4,1)S(1)} %broadcast_compare_fusion, bf16[256,2,80]{0,2,1:T(8,128)(2,1)S(1)} %bitcast.127, bf16[8192,2,80]{0,2,1:T(8,128)(2,1)} %bitcast.125), kind=kOutput, calls=%fused_computation.2 | convolution fusion | flops 683671040 | bytes 21579776 | tf_op jit(solution)/shard_map/rhd,khd->hrk/dot_general | solution.py:84
  108.0 0.0 copy-start.2
  108.0 5.7 %copy-done.2 = f32[2,256,8192]{2,1,0:T(8,128)} copy-done((f32[2,256,8192]{2,1,0:T(8,128)}, f32[2,256,8192]{2,1,0:T(8,128)S(1)}, u32[]{:S(2)}) %copy-start.2) | copy-done | bytes 16777240
  113.7 4.8 %fusion.2 = f32[2,256]{1,0:T(2,128)S(1)} fusion(f32[2,256,8192]{2,1,0:T(8,128)S(1)} %get-tuple-element.6, f32[2,256]{1,0:T(2,128)S(1)} %broadcast_maximum_fusion, pred[256,8192]{1,0:T(8,128)(4,1)S(1)} %broadcast_compare_fusion), kind=kLoop, calls=%fused_computation.5 | loop fusion | flops 16776704 | bytes 18878464 | tf_op jit(solution)/shard_map/reduce_sum | solution.py:90
  118.5 41.9 %all-gather.5.cloned.1.call-done = bf16[8192,160]{0,1:T(8,128)(2,1)} async-done(((bf16[256,160]{0,1:T(8,128)(2,1)}), bf16[8192,160]{0,1:T(8,128)(2,1)}) %all-gather.5.cloned.1.call-update) | async-done | bytes 2621456 | tf_op jit(solution)/shard_map/all_gather | solution.py:77
  160.4 0.0 copy-start.5
  160.4 8.5 %fusion.35 = bf16[256,2,80]{0,2,1:T(8,128)(2,1)S(1)} fusion(bf16[8192,2,80]{0,2,1:T(8,128)(2,1)} %bitcast.126, f32[2,256,8192]{2,1,0:T(8,128)} %copy-done.2, f32[2,256]{1,0:T(2,128)S(1)} %broadcast_maximum_fusion, pred[256,8192]{1,0:T(8,128)(4,1)S(1)} %broadcast_compare_fusion, f32[256,2]{0,1:T(2,128)S(1)} %bitcast.124), kind=kOutput, calls=%fused_computation.42 | convolution fusion | flops 687947776 | bytes 21581824 | tf_op jit(solution)/shard_map/hrk,khd->hrd/dot_general | solution.py:91
  168.9 0.0 copy-start.8
  168.9 0.0 copy-done.5
  168.9 1.2 convolution_convert_fusion
  170.2 0.0 all-reduce.2.cloned.1.call-update
  170.2 74.2 %all-reduce.2.cloned.1.call-done = bf16[256,1280]{1,0:T(8,128)(2,1)} async-done(((bf16[256,1280]{1,0:T(8,128)(2,1)}), bf16[256,1280]{1,0:T(8,128)(2,1)}) %all-reduce.2.cloned.1.call-update) | async-done | bytes 655376 | tf_op jit(solution)/shard_map/psum | solution.py:101
  244.4 0.0 copy-done
  244.4 1.5 fusion.44
  246.0 0.0 copy-done.8
  246.0 0.1 multiply_convert_fusion
  246.1 2.4 stack.8
  248.6 0.0 copy-start.4
  248.6 0.0 copy-start.11
  248.6 14.4 %all-to-all-start = ((bf16[32,256,256]{1,2,0:T(8,128)(2,1)}), bf16[32,256,256]{1,2,0:T(8,128)(2,1)}, u32[]{:S(2)}, u32[]{:S(2)}) async-start(bf16[32,256,256]{1,2,0:T(8,128)(2,1)} %stack.8), calls=%async_computation | async-start | bytes 8388608 | tf_op jit(solution)/shard_map/all_to_all | solution.py:117
  263.0 0.0 copy-done.4
  263.1 0.5 fusion.12
  263.5 0.0 copy-done.11
  263.6 0.0 copy-start.9
  263.6 0.0 copy-start.6
  263.6 0.0 copy-start.7
  263.6 4.7 %fusion.100 = (f32[128,512]{1,0:T(8,128)S(1)}, f32[128,512]{1,0:T(8,128)S(1)}) fusion(bf16[8192,512]{1,0:T(8,128)(2,1)} %param.20, bf16[128,8192]{1,0:T(8,128)(2,1)S(1)} %copy-done.4, f32[8192]{0:T(1024)S(1)} %copy-done.11, f32[128]{0:T(128)S(1)} %add_rsqrt_fusion.3), kind=kOutput, calls=%fused_computation.160 | convolution fusion | flops 1078001664 | bytes 11043328 | tf_op jit(solution)/shard_map/dot_general | solution.py:126
  268.3 0.1 mul.214
  268.4 0.2 reduce_sum.70
  268.6 0.1 fusion.73
  268.7 0.0 copy-done.9
  268.7 0.0 copy-done.6
  268.7 0.0 copy-done.7
  268.8 2.8 compare_and_fusion
  271.5 88.4 %all-to-all-done = bf16[32,256,256]{1,2,0:T(8,128)(2,1)} async-done(((bf16[32,256,256]{1,2,0:T(8,128)(2,1)}), bf16[32,256,256]{1,2,0:T(8,128)(2,1)}, u32[]{:S(2)}, u32[]{:S(2)}) %all-to-all-start) | async-done | bytes 4194336 | tf_op jit(solution)/shard_map/all_to_all | solution.py:117
  360.0 6.5 %copy.33 = bf16[32,256,256]{1,0,2:T(8,128)(2,1)} copy(bf16[32,256,256]{1,2,0:T(8,128)(2,1)} %all-to-all-done) | data formatting | bytes 8388608 | tf_op jit(solution)/shard_map/all_to_all | solution.py:117
  366.5 7.4 %reshape_reshape.3 = bf16[8192,1,2,128]{0,3,2,1:T(8,128)(2,1)} reshape(bf16[32,256,256]{1,0,2:T(8,128)(2,1)} %copy.33) | data formatting | bytes 8388608 | tf_op jit(solution)/shard_map/reshape;reshape | solution.py:132
  373.9 0.2 mul.215
  374.1 0.0 copy-start.3
  374.1 9.6 %fusion = (f32[4,128]{1,0:T(4,128)S(1)}, f32[8192,128,4]{1,0,2:T(8,128)}) fusion(pred[128,8192]{0,1:T(8,128)(4,1)S(1)} %compare_and_fusion, bf16[8192,1,2,128]{0,3,2,1:T(8,128)(2,1)} %reshape_reshape.3, f32[128,512]{1,0:T(8,128)S(1)} %get-tuple-element.8, f32[16,8,4,128]{3,2,1,0:T(4,128)S(1)} %bitcast.121, f32[512]{0:T(512)S(1)} %broadcast_bitcast_fusion), kind=kOutput, calls=%fused_computation.3 | convolution fusion | flops 1082392064 | bytes 20451328 | tf_op jit(solution)/shard_map/rgqd,kgd->gqrk/dot_general | solution.py:139
  383.7 0.0 copy-done.3
  383.7 0.0 copy-start.1
  383.7 7.5 %fusion.41 = bf16[128,1,4,128]{0,3,2,1:T(8,128)(2,1)S(1)} fusion(f32[8192,128,4]{1,0,2:T(8,128)} %get-tuple-element.10, pred[128,8192]{0,1:T(8,128)(4,1)S(1)} %compare_and_fusion, bf16[8192,1,2,128]{0,3,2,1:T(8,128)(2,1)S(1)} %copy-done.3, f32[128,4]{0,1:T(4,128)S(1)} %bitcast.128), kind=kOutput, calls=%fused_computation.44 | convolution fusion | flops 1082261504 | bytes 20056064 | tf_op jit(solution)/shard_map/gqrk,kgd->rgqd/dot_general | solution.py:144
  391.1 0.8 copy.39
  391.9 0.0 copy-done.1
  (11 shorter events, 0.1 us)
Async XLA Ops:
  6.5 237.9 %copy-start = (bf16[1280,256]{1,0:T(8,128)(2,1)S(1)}, bf16[1280,256]{1,0:T(8,128)(2,1)}, u32[]{:S(2)}) copy-start(bf16[1280,256]{1,0:T(8,128)(2,1)} %param.16) | copy-start | bytes 1966084
  6.5 30.2 %copy-start.10 = (bf16[3,1280,160]{1,2,0:T(8,128)(2,1)S(1)}, bf16[3,1280,160]{1,2,0:T(8,128)(2,1)}, u32[]{:S(2)}) copy-start(bf16[3,1280,160]{1,2,0:T(8,128)(2,1)} %param.14) | copy-start | bytes 3686404
  6.5 95.9 %all-gather.3.cloned.1.call-start = ((), (), s32[]{:S(2)}) async-start(), calls=%async_computation.1 | async-start | bytes 2703360 | tf_op jit(solution)/shard_map/all_gather | solution.py:76
  36.6 123.8 %all-gather.5.cloned.1.call-start = ((), (), s32[]{:S(2)}) async-start(), calls=%async_computation.2 | async-start | bytes 2703360 | tf_op jit(solution)/shard_map/all_gather | solution.py:77
  37.7 206.7 %all-reduce.2.cloned.1.call-start = ((), (), s32[]{:S(2)}) async-start(), calls=%async_computation.3 | async-start | bytes 1310720 | tf_op jit(solution)/shard_map/psum | solution.py:101
  108.0 5.7 %copy-start.2 = (f32[2,256,8192]{2,1,0:T(8,128)}, f32[2,256,8192]{2,1,0:T(8,128)S(1)}, u32[]{:S(2)}) copy-start(f32[2,256,8192]{2,1,0:T(8,128)S(1)} %get-tuple-element.6) | copy-start | bytes 50331652
  160.4 8.5 %copy-start.5 = (bf16[160,1280]{1,0:T(8,128)(2,1)S(1)}, bf16[160,1280]{1,0:T(8,128)(2,1)}, u32[]{:S(2)}) copy-start(bf16[160,1280]{1,0:T(8,128)(2,1)} %param.15) | copy-start | bytes 1228804
  168.9 77.1 %copy-start.8 = (f32[128]{0:T(128)S(1)}, f32[128]{0:T(128)}, u32[]{:S(2)}) copy-start(f32[128]{0:T(128)} %param.17) | copy-start | bytes 1540
  248.6 14.4 %copy-start.4 = (bf16[128,8192]{1,0:T(8,128)(2,1)S(1)}, bf16[128,8192]{1,0:T(8,128)(2,1)}, u32[]{:S(2)}) copy-start(bf16[128,8192]{1,0:T(8,128)(2,1)} %param.18) | copy-start | bytes 6291460
  248.6 15.0 %copy-start.11 = (f32[8192]{0:T(1024)S(1)}, f32[8192]{0:T(1024)}, u32[]{:S(2)}) copy-start(f32[8192]{0:T(1024)} %param.19) | copy-start | bytes 98308
  248.6 111.4 %all-to-all-start = ((bf16[32,256,256]{1,2,0:T(8,128)(2,1)}), bf16[32,256,256]{1,2,0:T(8,128)(2,1)}, u32[]{:S(2)}, u32[]{:S(2)}) async-start(bf16[32,256,256]{1,2,0:T(8,128)(2,1)} %stack.8), calls=%async_computation | async-start | bytes 8388608 | tf_op jit(solution)/shard_map/all_to_all | solution.py:117
  263.6 5.1 %copy-start.9 = (f32[128]{0:T(128)S(1)}, f32[128]{0:T(128)}, u32[]{:S(2)}) copy-start(f32[128]{0:T(128)} %param.21) | copy-start | bytes 1540
  263.6 5.2 %copy-start.6 = (s32[128]{0:T(128)S(1)}, s32[128]{0:T(128)}, u32[]{:S(2)}) copy-start(s32[128]{0:T(128)} %param.23) | copy-start | bytes 1540
  263.6 5.2 %copy-start.7 = (s32[128]{0:T(128)S(1)}, s32[128]{0:T(128)}, u32[]{:S(2)}) copy-start(s32[128]{0:T(128)} %param.22) | copy-start | bytes 1540
  374.1 9.6 %copy-start.3 = (bf16[8192,1,2,128]{0,3,2,1:T(8,128)(2,1)S(1)}, bf16[8192,1,2,128]{0,3,2,1:T(8,128)(2,1)}, u32[]{:S(2)}) copy-start(bf16[8192,1,2,128]{0,3,2,1:T(8,128)(2,1)} %reshape_reshape.3) | copy-start | bytes 12582916
  383.7 8.2 %copy-start.1 = (bf16[1280,256]{1,0:T(8,128)(2,1)S(1)}, bf16[1280,256]{1,0:T(8,128)(2,1)}, u32[]{:S(2)}) copy-start(bf16[1280,256]{1,0:T(8,128)(2,1)} %param.16) | copy-start | bytes 1966084
Sparse Core Ops, SparseCore 0:
  36.8 65.6 all-gather.2
  104.9 55.4 all-gather.4
  170.3 74.0 all-reduce.1
